TPU v7x, 256 devices: a whole 4x4x8 slice. The times are simulated.
256 devices in a mesh: row: 32 (over x_hi, z, core), col: 8 (over y, x_lo).
Axes of the slice: x: 4 (x_hi: 2, x_lo: 2; x = x_hi * 2 + x_lo), y: 4, z: 8, core: 2. Of those that a mesh axis runs over, the one named last changes fastest.
Arguments:
- p_tiles: bfloat16 [1024, 2, 128, 128], P(('row', 'col')), may hold values from -0.5 to 0.5
- p_cols: int32 [1024, 2], P(('row', 'col')), may hold values from 0 to 31, as said below
- q_tiles: bfloat16 [1024, 6, 128, 128], P(('row', 'col')), may hold values from -1.796875 to 1.796875
- q_cols: int32 [1024, 6], P(('row', 'col')), may hold values from 0 to 31, all different within a row
Outputs:
- coarse: float32 [4096, 4096], P('row', 'col')
Inputs may be any that keep to these rules, and one draw needn't show every extreme that they name: `p_cols`: the 2 coarse tiles in one row differ; among the fine blocks held by the devices of one index of col, every coarse tile is named at least once and at most 16 times, and some tile exactly 16 times. `q_cols`: the 6 coarse tiles in one row differ; every coarse tile appears somewhere.
All inputs are finite; a program needn't handle non-finite values.
Results may differ from a plain program's by a relative error of at most 0.0003.
Values may be sent and summed in bfloat16 or wider, within the bound.
A program may use at most 128 MiB of HBM per device.

v0:
```python
import math
import jax
import jax.numpy as jnp
from jax import lax
from jax.sharding import PartitionSpec as P


def spread_tiles(tile_set, columns, tile_count):
    blocks, per_block, extent, _ = tile_set.shape
    flipped = jnp.swapaxes(tile_set, 2, 3)
    fine_ids = jnp.broadcast_to(jnp.arange(blocks, dtype=jnp.int32)[:, None], (blocks, per_block))
    placed = jnp.zeros((tile_count, extent, blocks, extent), tile_set.dtype)
    placed = placed.at[columns, :, fine_ids, :].set(flipped)
    return placed.reshape(tile_count * extent, blocks * extent)


def fold_tiles(summed, transposed, tile_set, columns):
    blocks, per_block, extent, _ = tile_set.shape
    height = transposed.shape[0]
    bundle = math.gcd(blocks, 8)
    tile_groups = tile_set.reshape(blocks // bundle, bundle, per_block, extent, extent)
    column_groups = columns.reshape(blocks // bundle, bundle * per_block)

    def one_group(running, inputs):
        position, bundle_tiles, coarse_ids = inputs
        offset = position * bundle * extent
        stripe = lax.dynamic_slice_in_dim(transposed, offset, bundle * extent, 1).reshape(
            height, bundle, extent
        )
        product = jnp.einsum(
            "rfa,fkab->rfkb", stripe, bundle_tiles, preferred_element_type=jnp.float32
        )
        tiled = running.reshape(height, -1, extent)
        tiled = tiled.at[:, coarse_ids, :].add(product.reshape(height, bundle * per_block, extent))
        return (tiled.reshape(height, -1), None)

    counter = jnp.arange(blocks // bundle, dtype=jnp.int32)
    summed, _ = lax.scan(one_group, summed, (counter, tile_groups, column_groups))
    return summed


def body(p_tiles, p_cols, q_tiles, q_cols):
    extent = p_tiles.shape[2]
    tile_count = lax.axis_size("row")
    expanded = spread_tiles(p_tiles, p_cols, tile_count)
    transposed = lax.all_to_all(expanded, "row", split_axis=0, concat_axis=1, tiled=True)
    empty = jnp.zeros((transposed.shape[0], tile_count * extent), jnp.float32)
    partial_sum = fold_tiles(
        empty,
        transposed,
        lax.all_gather(q_tiles, "row", axis=0, tiled=True),
        lax.all_gather(q_cols, "row", axis=0, tiled=True),
    )
    return lax.psum_scatter(partial_sum, "col", scatter_dimension=1, tiled=True)


def solution(mesh):
    placed = (
        P(("row", "col"), None, None, None),
        P(("row", "col"), None),
        P(("row", "col"), None, None, None),
        P(("row", "col"), None),
    )
    return jax.shard_map(
        body, mesh=mesh, in_specs=placed, out_specs=P("row", "col"), check_vma=False
    )
```

profile of v0, /device:TPU:1, one launch (start us, length us, event | category | flops | bytes accessed | tf_op | source)
XLA Modules:
  0.0 604.4 jit_solution(11690526982969184347)
XLA Ops:
  9.3 3.0 broadcast_in_dim.18
  14.5 6.5 %copy.24 = bf16[32,128,4,128]{1,3,2,0:T(8,128)(2,1)} copy(bf16[32,128,4,128]{3,1,2,0:T(8,128)(2,1)} %scatter_fusion.1) | data formatting | bytes 8388608 | tf_op jit(solution)/shard_map/scatter | solution.py:13
  21.0 12.8 %all-to-all-start = ((bf16[32,128,512]{1,2,0:T(8,128)(2,1)}), bf16[32,128,512]{1,2,0:T(8,128)(2,1)}, u32[]{:S(2)}, u32[]{:S(2)}) async-start(bf16[32,128,512]{1,2,0:T(8,128)(2,1)} %bitcast.65), calls=%async_computation | async-start | bytes 8388608 | tf_op jit(solution)/shard_map/all_to_all | solution.py:46
  33.8 154.7 %all-gather = s32[32,4,6]{2,1,0:T(4,128)S(1)} all-gather(s32[1,4,6]{2,1,0:T(4,128)S(1)} %bitcast.68), channel_id=1, replica_groups=mesh['row'=32,'col'=8] {'row'}, dimensions={0}, use_global_device_ids=true | all-gather | bytes 3168 | tf_op jit(solution)/shard_map/all_gather | solution.py:52
  188.6 77.6 %all-gather.3.cloned.1.call-done = bf16[128,6,128,128]{3,2,1,0:T(8,128)(2,1)} async-done(((bf16[4,6,128,128]{3,2,1,0:T(8,128)(2,1)}), bf16[128,6,128,128]{3,2,1,0:T(8,128)(2,1)}) %all-gather.3.cloned.1.call-update) | async-done | bytes 25165840 | tf_op jit(solution)/shard_map/all_gather | solution.py:51
  267.7 274.9 %while.12 = (s32[]{:T(128)}, f32[128,4096]{0,1:T(8,128)}, s32[16,48]{1,0:T(8,128)S(1)}, bf16[16,8,6,128,128]{4,3,2,1,0:T(8,128)(2,1)}, s32[16]{0:T(128)S(1)}, /*...) while((s32[]{:T(128)}, f32[128,4096]{0,1:T(8,128)}, ...), condition=%wide.region_3.4_spmd, body=%wide.region_1.3_spmd.sunk | while | flops 202113168 | bytes 29623528 | solution.py:38
  276.3 6.7 %scatter_fusion = f32[128,32,128]{2,0,1:T(8,128)S(1)} fusion(f32[128,32,128]{2,0,1:T(8,128)S(1)} %copy.34, s32[48]{0:T(128)S(1)} %fusion.16, f32[48,128,128]{2,1,0:T(8,128)} %bitcast.61), kind=kCustom, calls=%fused_computation.clone.1 | custom fusion | flops 786432 | bytes 9437376 | tf_op jit(solution)/shard_map/while/body/eval_jaxpr/scatter-add | solution.py:34
  293.5 6.7 %scatter_fusion = f32[128,32,128]{2,0,1:T(8,128)S(1)} fusion(f32[128,32,128]{2,0,1:T(8,128)S(1)} %copy.34, s32[48]{0:T(128)S(1)} %fusion.16, f32[48,128,128]{2,1,0:T(8,128)} %bitcast.61), kind=kCustom, calls=%fused_computation.clone.1 | custom fusion | flops 786432 | bytes 9437376 | tf_op jit(solution)/shard_map/while/body/eval_jaxpr/scatter-add | solution.py:34
  310.7 6.7 %scatter_fusion = f32[128,32,128]{2,0,1:T(8,128)S(1)} fusion(f32[128,32,128]{2,0,1:T(8,128)S(1)} %copy.34, s32[48]{0:T(128)S(1)} %fusion.16, f32[48,128,128]{2,1,0:T(8,128)} %bitcast.61), kind=kCustom, calls=%fused_computation.clone.1 | custom fusion | flops 786432 | bytes 9437376 | tf_op jit(solution)/shard_map/while/body/eval_jaxpr/scatter-add | solution.py:34
  327.8 6.7 %scatter_fusion = f32[128,32,128]{2,0,1:T(8,128)S(1)} fusion(f32[128,32,128]{2,0,1:T(8,128)S(1)} %copy.34, s32[48]{0:T(128)S(1)} %fusion.16, f32[48,128,128]{2,1,0:T(8,128)} %bitcast.61), kind=kCustom, calls=%fused_computation.clone.1 | custom fusion | flops 786432 | bytes 9437376 | tf_op jit(solution)/shard_map/while/body/eval_jaxpr/scatter-add | solution.py:34
  345.0 6.7 %scatter_fusion = f32[128,32,128]{2,0,1:T(8,128)S(1)} fusion(f32[128,32,128]{2,0,1:T(8,128)S(1)} %copy.34, s32[48]{0:T(128)S(1)} %fusion.16, f32[48,128,128]{2,1,0:T(8,128)} %bitcast.61), kind=kCustom, calls=%fused_computation.clone.1 | custom fusion | flops 786432 | bytes 9437376 | tf_op jit(solution)/shard_map/while/body/eval_jaxpr/scatter-add | solution.py:34
  362.2 6.7 %scatter_fusion = f32[128,32,128]{2,0,1:T(8,128)S(1)} fusion(f32[128,32,128]{2,0,1:T(8,128)S(1)} %copy.34, s32[48]{0:T(128)S(1)} %fusion.16, f32[48,128,128]{2,1,0:T(8,128)} %bitcast.61), kind=kCustom, calls=%fused_computation.clone.1 | custom fusion | flops 786432 | bytes 9437376 | tf_op jit(solution)/shard_map/while/body/eval_jaxpr/scatter-add | solution.py:34
  379.4 6.7 %scatter_fusion = f32[128,32,128]{2,0,1:T(8,128)S(1)} fusion(f32[128,32,128]{2,0,1:T(8,128)S(1)} %copy.34, s32[48]{0:T(128)S(1)} %fusion.16, f32[48,128,128]{2,1,0:T(8,128)} %bitcast.61), kind=kCustom, calls=%fused_computation.clone.1 | custom fusion | flops 786432 | bytes 9437376 | tf_op jit(solution)/shard_map/while/body/eval_jaxpr/scatter-add | solution.py:34
  396.6 6.7 %scatter_fusion = f32[128,32,128]{2,0,1:T(8,128)S(1)} fusion(f32[128,32,128]{2,0,1:T(8,128)S(1)} %copy.34, s32[48]{0:T(128)S(1)} %fusion.16, f32[48,128,128]{2,1,0:T(8,128)} %bitcast.61), kind=kCustom, calls=%fused_computation.clone.1 | custom fusion | flops 786432 | bytes 9437376 | tf_op jit(solution)/shard_map/while/body/eval_jaxpr/scatter-add | solution.py:34
  413.7 6.7 %scatter_fusion = f32[128,32,128]{2,0,1:T(8,128)S(1)} fusion(f32[128,32,128]{2,0,1:T(8,128)S(1)} %copy.34, s32[48]{0:T(128)S(1)} %fusion.16, f32[48,128,128]{2,1,0:T(8,128)} %bitcast.61), kind=kCustom, calls=%fused_computation.clone.1 | custom fusion | flops 786432 | bytes 9437376 | tf_op jit(solution)/shard_map/while/body/eval_jaxpr/scatter-add | solution.py:34
  430.9 6.7 %scatter_fusion = f32[128,32,128]{2,0,1:T(8,128)S(1)} fusion(f32[128,32,128]{2,0,1:T(8,128)S(1)} %copy.34, s32[48]{0:T(128)S(1)} %fusion.16, f32[48,128,128]{2,1,0:T(8,128)} %bitcast.61), kind=kCustom, calls=%fused_computation.clone.1 | custom fusion | flops 786432 | bytes 9437376 | tf_op jit(solution)/shard_map/while/body/eval_jaxpr/scatter-add | solution.py:34
  448.1 6.7 %scatter_fusion = f32[128,32,128]{2,0,1:T(8,128)S(1)} fusion(f32[128,32,128]{2,0,1:T(8,128)S(1)} %copy.34, s32[48]{0:T(128)S(1)} %fusion.16, f32[48,128,128]{2,1,0:T(8,128)} %bitcast.61), kind=kCustom, calls=%fused_computation.clone.1 | custom fusion | flops 786432 | bytes 9437376 | tf_op jit(solution)/shard_map/while/body/eval_jaxpr/scatter-add | solution.py:34
  465.3 6.7 %scatter_fusion = f32[128,32,128]{2,0,1:T(8,128)S(1)} fusion(f32[128,32,128]{2,0,1:T(8,128)S(1)} %copy.34, s32[48]{0:T(128)S(1)} %fusion.16, f32[48,128,128]{2,1,0:T(8,128)} %bitcast.61), kind=kCustom, calls=%fused_computation.clone.1 | custom fusion | flops 786432 | bytes 9437376 | tf_op jit(solution)/shard_map/while/body/eval_jaxpr/scatter-add | solution.py:34
  482.5 6.7 %scatter_fusion = f32[128,32,128]{2,0,1:T(8,128)S(1)} fusion(f32[128,32,128]{2,0,1:T(8,128)S(1)} %copy.34, s32[48]{0:T(128)S(1)} %fusion.16, f32[48,128,128]{2,1,0:T(8,128)} %bitcast.61), kind=kCustom, calls=%fused_computation.clone.1 | custom fusion | flops 786432 | bytes 9437376 | tf_op jit(solution)/shard_map/while/body/eval_jaxpr/scatter-add | solution.py:34
  499.6 6.7 %scatter_fusion = f32[128,32,128]{2,0,1:T(8,128)S(1)} fusion(f32[128,32,128]{2,0,1:T(8,128)S(1)} %copy.34, s32[48]{0:T(128)S(1)} %fusion.16, f32[48,128,128]{2,1,0:T(8,128)} %bitcast.61), kind=kCustom, calls=%fused_computation.clone.1 | custom fusion | flops 786432 | bytes 9437376 | tf_op jit(solution)/shard_map/while/body/eval_jaxpr/scatter-add | solution.py:34
  516.8 6.7 %scatter_fusion = f32[128,32,128]{2,0,1:T(8,128)S(1)} fusion(f32[128,32,128]{2,0,1:T(8,128)S(1)} %copy.34, s32[48]{0:T(128)S(1)} %fusion.16, f32[48,128,128]{2,1,0:T(8,128)} %bitcast.61), kind=kCustom, calls=%fused_computation.clone.1 | custom fusion | flops 786432 | bytes 9437376 | tf_op jit(solution)/shard_map/while/body/eval_jaxpr/scatter-add | solution.py:34
  534.0 6.7 %scatter_fusion = f32[128,32,128]{2,0,1:T(8,128)S(1)} fusion(f32[128,32,128]{2,0,1:T(8,128)S(1)} %copy.34, s32[48]{0:T(128)S(1)} %fusion.16, f32[48,128,128]{2,1,0:T(8,128)} %bitcast.61), kind=kCustom, calls=%fused_computation.clone.1 | custom fusion | flops 786432 | bytes 9437376 | tf_op jit(solution)/shard_map/while/body/eval_jaxpr/scatter-add | solution.py:34
  542.6 2.9 copy.26
  545.5 52.1 %reduce-scatter.2.cloned.1.call-done = f32[128,512]{1,0:T(8,128)} async-done(((f32[128,4096]{1,0:T(8,128)}), f32[128,512]{1,0:T(8,128)}) %reduce-scatter.2.cloned.1.call-update) | async-done | bytes 262160 | tf_op jit(solution)/shard_map/reduce_scatter | solution.py:54
  (127 shorter events, 163.2 us)
Async XLA Ops:
  6.5 259.7 %all-gather.3.cloned.1.call-start = ((), (), s32[]{:S(2)}) async-start(), calls=%async_computation.2 | async-start | bytes 25952256 | tf_op jit(solution)/shard_map/all_gather | solution.py:51
  21.0 12.8 %copy-start = (s32[4,6]{1,0:T(4,128)S(1)}, s32[4,6]{1,0:T(4,128)}, u32[]{:S(2)}) copy-start(s32[4,6]{1,0:T(4,128)} %param.9) | copy-start | bytes 292
  21.0 167.6 %all-to-all-start = ((bf16[32,128,512]{1,2,0:T(8,128)(2,1)}), bf16[32,128,512]{1,2,0:T(8,128)(2,1)}, u32[]{:S(2)}, u32[]{:S(2)}) async-start(bf16[32,128,512]{1,2,0:T(8,128)(2,1)} %bitcast.65), calls=%async_computation | async-start | bytes 8388608 | tf_op jit(solution)/shard_map/all_to_all | solution.py:46
  33.8 563.8 %reduce-scatter.2.cloned.1.call-start = ((), (), s32[]{:S(2)}) async-start(), calls=%async_computation.3 | async-start | bytes 2359296 | tf_op jit(solution)/shard_map/reduce_scatter | solution.py:54
Sparse Core Ops, SparseCore 0:
  10.1 256.0 all-gather.2
  545.6 51.9 reduce-scatter.1
where the time goes:
time: 608 us; the launch traced here: 604 us
  blocking collectives  155 us (25%)
  local copies, waits for them, and re-layouts  141 us (23%)
  waiting for transfers between devices  130 us (21%)
  other arithmetic  109 us (18%)
  matrix products  33 us (5%)
  between operations  13.4 us (2%)
  starting transfers between devices  12.8 us (2%)
  loops' own time  10.5 us (2%)
    all_gather x1, blocking collectives, body(): lax.all_gather(q_cols, 'row', axis=0, tiled=True)  155 us
    scatter-add x16, other arithmetic, one_group(): tiled.at[:, coarse_ids, :]  108 us
    all_gather x1, waiting for transfers between devices, body(): lax.all_gather(q_tiles, 'row', axis=0, tiled=True)  77.6 us
    reduce_scatter x1, waiting for transfers between devices, body(): return lax.psum_scatter(partial_sum, 'col', scatter_dimension=1, tiled=True)  52.1 us
    reshape x16, local copies, waits for them, and re-layouts, one_group(): product.reshape(height, bundle * per_block, extent)  37.8 us
    dot_general x16, matrix products, one_group(): jnp.einsum('rfa,fkab->rfkb', stripe, bundle_tiles, preferred_element_type...  33 us
    reshape x16, local copies, waits for them, and re-layouts, one_group(): tiled = running.reshape(height, -1, extent)  30.7 us
    scatter-add x16, local copies, waits for them, and re-layouts, one_group(): tiled.at[:, coarse_ids, :]  29.2 us
  transfers between devices with their start and end apart: 3, of which 2 were waited for; matrix products, arithmetic and copies ran while one was open for 2% of the time, Pallas kernels for 0%

commit v1 on v0

--- a/solution.py
+++ b/solution.py
@@ -3,6 +3,11 @@
 import jax.numpy as jnp
 from jax import lax
 from jax.sharding import PartitionSpec as P
+
+
+def all_by_exchange(x, axis, along):
+    sent = jnp.stack([x] * lax.axis_size(axis))
+    return jnp.concatenate(lax.all_to_all(sent, axis, 0, 0), axis=along)
 
 
 def spread_tiles(tile_set, columns, tile_count):
@@ -48,7 +53,7 @@
     partial_sum = fold_tiles(
         empty,
         transposed,
-        lax.all_gather(q_tiles, "row", axis=0, tiled=True),
+        all_by_exchange(q_tiles, "row", 0),
         lax.all_gather(q_cols, "row", axis=0, tiled=True),
     )
     return lax.psum_scatter(partial_sum, "col", scatter_dimension=1, tiled=True)

time: 608 us -> 1080 us (1.78)
  blocking collectives: 155 us -> 593 us
  waiting for transfers between devices: 130 us -> 144 us
  local copies, waits for them, and re-layouts: 141 us -> 153 us
    all_gather x1, blocking collectives: 155 us -> 593 us  [body(): lax.all_gather(q_cols, 'row', axis=0, tiled=True)]
    all_to_all x1, waiting for transfers between devices: 0.01 us -> 95.8 us  [body(): lax.all_to_all(expanded, 'row', split_axis=0, concat_axis=1, tiled=True)]
    all_gather x1 -> x0, waiting for transfers between devices: 77.6 us -> none  [body(): lax.all_gather(q_tiles, 'row', axis=0, tiled=True)]
  transfers between devices with their start and end apart: 3 -> 3, of which waited for: 2 -> 2; matrix products, arithmetic and copies ran while one was open for 2% -> 0% of each run, Pallas kernels for 0% -> 0%
where the time goes in v1:
time: 1080 us; the launch traced here: 1070 us
  blocking collectives  593 us (55%)
  local copies, waits for them, and re-layouts  153 us (14%)
  waiting for transfers between devices  144 us (13%)
  other arithmetic  109 us (10%)
  matrix products  31.6 us (3%)
  starting transfers between devices  20.2 us (2%)
  between operations  13.5 us (1%)
    all_gather x1, blocking collectives, body(): lax.all_gather(q_cols, 'row', axis=0, tiled=True)  593 us
    scatter-add x16, other arithmetic, one_group(): tiled.at[:, coarse_ids, :]  108 us
    all_to_all x1, waiting for transfers between devices, body(): lax.all_to_all(expanded, 'row', split_axis=0, concat_axis=1, tiled=True)  95.8 us
    reduce_scatter x1, waiting for transfers between devices, body(): return lax.psum_scatter(partial_sum, 'col', scatter_dimension=1, tiled=True)  48.6 us
    reshape x16, local copies, waits for them, and re-layouts, one_group(): product.reshape(height, bundle * per_block, extent)  39.3 us
    dot_general x16, matrix products, one_group(): jnp.einsum('rfa,fkab->rfkb', stripe, bundle_tiles, preferred_element_type...  31.6 us
    reshape x16, local copies, waits for them, and re-layouts, one_group(): tiled = running.reshape(height, -1, extent)  30.7 us
    scatter-add x16, local copies, waits for them, and re-layouts, one_group(): tiled.at[:, coarse_ids, :]  30.7 us
  transfers between devices with their start and end apart: 3, of which 2 were waited for; matrix products, arithmetic and copies ran while one was open for 0% of the time, Pallas kernels for 0%

profile of v1, /device:TPU:1, one launch (start us, length us, event | category | flops | bytes accessed | tf_op | source)
XLA Modules:
  0.0 1073.2 jit_solution(12527763792433293843)
XLA Ops:
  13.9 6.5 copy.25
  20.3 12.7 %all-to-all-start.1 = ((bf16[32,128,512]{1,2,0:T(8,128)(2,1)}), bf16[32,128,512]{1,2,0:T(8,128)(2,1)}, u32[]{:S(2)}, u32[]{:S(2)}) async-start(bf16[32,128,512]{1,2,0:T(8,128)(2,1)} %bitcast.64), calls=%async_computation.1 | async-start | bytes 8388608 | tf_op jit(solution)/shard_map/all_to_all | solution.py:51
  33.5 95.8 %all-to-all-done.1 = bf16[32,128,512]{1,2,0:T(8,128)(2,1)} async-done(((bf16[32,128,512]{1,2,0:T(8,128)(2,1)}), bf16[32,128,512]{1,2,0:T(8,128)(2,1)}, u32[]{:S(2)}, u32[]{:S(2)}) %all-to-all-start.1) | async-done | bytes 4194336 | tf_op jit(solution)/shard_map/all_to_all | solution.py:51
  129.2 9.2 stack.2
  138.4 7.4 all-to-all-start
  145.9 592.5 %all-gather = s32[32,4,6]{2,1,0:T(4,128)S(1)} all-gather(s32[1,4,6]{2,1,0:T(4,128)S(1)} %bitcast.66), channel_id=1, replica_groups=mesh['row'=32,'col'=8] {'row'}, dimensions={0}, use_global_device_ids=true | all-gather | bytes 3168 | tf_op jit(solution)/shard_map/all_gather | solution.py:57
  740.1 274.8 %while.12 = (s32[]{:T(128)}, f32[128,4096]{0,1:T(8,128)}, s32[16,48]{1,0:T(8,128)S(1)}, bf16[16,8,6,128,128]{3,4,2,1,0:T(8,128)(2,1)}, s32[16]{0:T(128)S(1)}, /*...) while((s32[]{:T(128)}, f32[128,4096]{0,1:T(8,128)}, ...), condition=%wide.region_3.4_spmd, body=%wide.region_1.3_spmd.sunk | while | flops 202113168 | bytes 29623528 | solution.py:43
  748.6 6.7 scatter_fusion
  765.8 6.7 scatter_fusion
  783.0 6.7 scatter_fusion
  800.1 6.7 scatter_fusion
  817.3 6.7 scatter_fusion
  834.5 6.7 scatter_fusion
  851.7 6.7 scatter_fusion
  868.8 6.7 scatter_fusion
  886.0 6.7 scatter_fusion
  903.2 6.7 scatter_fusion
  920.4 6.7 scatter_fusion
  937.5 6.7 scatter_fusion
  954.7 6.7 scatter_fusion
  971.9 6.7 scatter_fusion
  989.1 6.7 scatter_fusion
  1006.2 6.7 scatter_fusion
  1017.8 48.6 %reduce-scatter.2.cloned.1.call-done = f32[128,512]{1,0:T(8,128)} async-done(((f32[128,4096]{1,0:T(8,128)}), f32[128,512]{1,0:T(8,128)}) %reduce-scatter.2.cloned.1.call-update) | async-done | bytes 262160 | tf_op jit(solution)/shard_map/reduce_scatter | solution.py:59
  (130 shorter events, 169.7 us)
Async XLA Ops:
  20.3 12.7 %copy-start = (bf16[4,6,128,128]{3,2,1,0:T(8,128)(2,1)S(1)}, bf16[4,6,128,128]{3,2,1,0:T(8,128)(2,1)}, u32[]{:S(2)}) copy-start(bf16[4,6,128,128]{3,2,1,0:T(8,128)(2,1)} %param.8) | copy-start | bytes 2359300
  20.3 108.9 %all-to-all-start.1 = ((bf16[32,128,512]{1,2,0:T(8,128)(2,1)}), bf16[32,128,512]{1,2,0:T(8,128)(2,1)}, u32[]{:S(2)}, u32[]{:S(2)}) async-start(bf16[32,128,512]{1,2,0:T(8,128)(2,1)} %bitcast.64), calls=%async_computation.1 | async-start | bytes 8388608 | tf_op jit(solution)/shard_map/all_to_all | solution.py:51
  138.4 7.5 copy-start.1
  138.4 600.1 %all-to-all-start = ((bf16[32,4,6,128,128]{3,4,2,1,0:T(8,128)(2,1)}), bf16[32,4,6,128,128]{3,4,2,1,0:T(8,128)(2,1)}, u32[]{:S(2)}, u32[]{:S(2)}) async-start(bf16[32,4,6,128,128]{3,4,2,1,0:T(8,128)(2,1)} %stack.2), calls=%async_computation | async-start | bytes 50331648 | tf_op jit(solution)/shard_map/all_to_all | solution.py:10
  145.8 920.6 %reduce-scatter.2.cloned.1.call-start = ((), (), s32[]{:S(2)}) async-start(), calls=%async_computation.3 | async-start | bytes 2359296 | tf_op jit(solution)/shard_map/reduce_scatter | solution.py:59
Sparse Core Ops, SparseCore 0:
  1018.0 48.3 reduce-scatter.1
